TPU v7x, 32 devices: a whole 2x2x4 slice. The times are simulated.
32 devices in a mesh: rep: 8 (over z, y), shard: 4 (over x, core).
Axes of the slice: x: 2, y: 2, z: 4, core: 2. Of those that a mesh axis runs over, the one named last changes fastest.
Arguments:
- tokens: bfloat16 [4096, 1024], P(('rep', 'shard')), may hold values from -6 to 6
- cotangent: bfloat16 [4096, 1024], P(('rep', 'shard')), may hold values from -6 to 6
- doc_ids: int32 [4096], P(('rep', 'shard')), may hold values from -1 to 15, as said below
- w_query: bfloat16 [1024, 1024], P('shard'), may hold values from -0.1875 to 0.1875
- w_key: bfloat16 [1024, 512], P('shard'), may hold values from -0.1875 to 0.1875
- w_value: bfloat16 [1024, 512], P('shard'), may hold values from -0.1875 to 0.1875
- w_out: bfloat16 [1024, 1024], P('shard'), may hold values from -0.5 to 0.5
- w_gate: bfloat16 [1024, 4608], P('shard'), may hold values from -0.1875 to 0.1875
- w_up: bfloat16 [1024, 4608], P('shard'), may hold values from -0.1875 to 0.1875
- w_down: bfloat16 [4608, 1024], P('shard'), may hold values from -0.09375 to 0.09375
- gain_attn: bfloat16 [1024], P('shard'), may hold values from 0.5 to 1.5
- gain_ffn: bfloat16 [1024], P('shard'), may hold values from 0.5 to 1.5
- gain_query: bfloat16 [64], P('shard'), may hold values from 0.5 to 1.5
- gain_key: bfloat16 [64], P('shard'), may hold values from 0.5 to 1.5
Outputs:
- block_out: bfloat16 [4096, 1024], P(('rep', 'shard'))
- grad_tokens: float32 [4096, 1024], P(('rep', 'shard'))
- grad_w_query: float32 [1024, 1024], P('shard')
- grad_w_key: float32 [1024, 512], P('shard')
- grad_w_value: float32 [1024, 512], P('shard')
- grad_w_out: float32 [1024, 1024], P('shard')
- grad_w_gate: float32 [1024, 4608], P('shard')
- grad_w_up: float32 [1024, 4608], P('shard')
- grad_w_down: float32 [4608, 1024], P('shard')
- grad_gain_attn: float32 [1024], P('shard')
- grad_gain_ffn: float32 [1024], P('shard')
- grad_gain_query: float32 [64], P('shard')
- grad_gain_key: float32 [64], P('shard')
Inputs may be any that keep to these rules, and one draw needn't show every extreme that they name: `doc_ids`: each device's 128 slots hold its sequences one after another, numbered from 0 upward without gaps, followed by its empty slots marked -1; at least one device has no empty slot and holds 16 sequences.
All inputs are finite; a program needn't handle non-finite values.
Results may differ from a plain program's by a relative error of at most 0.02.
Values may be sent and summed in bfloat16 or wider, within the bound.
A program may use at most 192 MiB of HBM per device.

v0:
```python
import math
import jax
import jax.numpy as jnp
from jax import lax
from jax.sharding import PartitionSpec as P

QH = 16
KVH = 8
HEAD_DIM = 64
NORM_EPSILON = 1e-05
ROPE_BASE = 1000000.0


def matmul(left, right):
    return jnp.dot(left, right, preferred_element_type=jnp.float32)


def norm_rows(values, gain_vec):
    inv_rms = lax.rsqrt(jnp.mean(values * values, axis=-1, keepdims=True) + NORM_EPSILON)
    normed = values * inv_rms
    return (normed * gain_vec.astype(jnp.float32), normed, inv_rms)


def norm_back(grad_out, normed, inv_rms, gain_vec):
    scaled = grad_out * gain_vec.astype(jnp.float32)
    grad_in = inv_rms * (scaled - normed * jnp.mean(scaled * normed, axis=-1, keepdims=True))
    lead_axes = tuple(range(grad_out.ndim - 1))
    return (grad_in, jnp.sum(grad_out * normed, axis=lead_axes))


def doc_tables(doc_rows):
    block_len = doc_rows.shape[-1]
    row_index = jnp.arange(block_len)[:, None]
    col_index = jnp.arange(block_len)[None, :]
    same_doc = doc_rows[:, :, None] == doc_rows[:, None, :]
    allowed = same_doc & (row_index >= col_index)[None]
    earlier = same_doc & (row_index > col_index)[None]
    positions = jnp.sum(earlier.astype(jnp.int32), axis=2)
    return (allowed, positions)


def rope_tables(positions, head_dim):
    half_dim = head_dim // 2
    inv_freq = jnp.exp(
        jnp.arange(half_dim).astype(jnp.float32) * (-2.0 * math.log(ROPE_BASE) / head_dim)
    )
    angles = positions.astype(jnp.float32)[:, :, None, None] * inv_freq
    return (jnp.cos(angles), jnp.sin(angles))


def rotate(values, cos_tab, sin_tab):
    half_dim = values.shape[-1] // 2
    part_one = values[..., :half_dim]
    part_two = values[..., half_dim:]
    return jnp.concatenate(
        [part_one * cos_tab - part_two * sin_tab, part_two * cos_tab + part_one * sin_tab], axis=-1
    )


def rotate_back(values, cos_tab, sin_tab):
    half_dim = values.shape[-1] // 2
    part_one = values[..., :half_dim]
    part_two = values[..., half_dim:]
    return jnp.concatenate(
        [part_one * cos_tab + part_two * sin_tab, part_two * cos_tab - part_one * sin_tab], axis=-1
    )


def attn_probs_of(query_bf, key_bf, key_mask, log_total, score_scale):
    scores = (
        jnp.einsum("gqkrd,gskd->gkrqs", query_bf, key_bf, preferred_element_type=jnp.float32)
        * score_scale
    )
    if log_total is None:
        log_total = jnp.log(
            jnp.sum(jnp.where(key_mask, jnp.exp(scores), 0.0), axis=-1, keepdims=True)
        )
    return (jnp.where(key_mask, jnp.exp(scores - log_total), 0.0), log_total)


def local(
    tokens,
    cotangent,
    doc_ids,
    w_query,
    w_key,
    w_value,
    w_out,
    w_gate,
    w_up,
    w_down,
    gain_attn,
    gain_ffn,
    gain_query,
    gain_key,
):
    tok_rows = tokens.shape[0]
    head_share = QH // KVH
    score_scale = 1.0 / math.sqrt(HEAD_DIM)
    doc_rows = doc_ids[None, :]
    allowed, positions = doc_tables(doc_rows)
    key_mask = allowed[:, None, None]
    cos_tab, sin_tab = rope_tables(positions, HEAD_DIM)
    attn_set = (
        lax.all_gather(w_query, "shard", axis=0, tiled=True),
        lax.all_gather(w_key, "shard", axis=0, tiled=True),
        lax.all_gather(w_value, "shard", axis=0, tiled=True),
        lax.all_gather(w_out, "shard", axis=0, tiled=True),
        lax.all_gather(gain_attn, "shard", axis=0, tiled=True),
        lax.all_gather(gain_query, "shard", axis=0, tiled=True),
        lax.all_gather(gain_key, "shard", axis=0, tiled=True),
    )
    full_query, full_key, full_value, full_out, full_gattn, full_gquery, full_gkey = attn_set
    resid_in = tokens.astype(jnp.float32)
    normed_in, unit_in, rms_in = norm_rows(resid_in, full_gattn)
    normed_bf = normed_in.astype(jnp.bfloat16)
    query_raw = matmul(normed_bf, full_query).reshape(1, tok_rows, QH, HEAD_DIM)
    key_raw = matmul(normed_bf, full_key).reshape(1, tok_rows, KVH, HEAD_DIM)
    value_bf = (
        matmul(normed_bf, full_value).astype(jnp.bfloat16).reshape(1, tok_rows, KVH, HEAD_DIM)
    )
    query_normed, query_unit, query_rms = norm_rows(query_raw, full_gquery)
    key_normed, key_unit, key_rms = norm_rows(key_raw, full_gkey)
    query_bf = (
        rotate(query_normed, cos_tab, sin_tab)
        .astype(jnp.bfloat16)
        .reshape(1, tok_rows, KVH, head_share, HEAD_DIM)
    )
    key_bf = rotate(key_normed, cos_tab, sin_tab).astype(jnp.bfloat16)
    attn_probs, log_total = attn_probs_of(query_bf, key_bf, key_mask, None, score_scale)
    mixed_bf = (
        jnp.einsum(
            "gkrqs,gskd->gqkrd",
            attn_probs.astype(jnp.bfloat16),
            value_bf,
            preferred_element_type=jnp.float32,
        )
        .astype(jnp.bfloat16)
        .reshape(tok_rows, QH * HEAD_DIM)
    )
    resid_mid = resid_in + matmul(mixed_bf, full_out)
    ffn_set = (
        lax.all_gather(w_gate, "shard", axis=0, tiled=True),
        lax.all_gather(w_up, "shard", axis=0, tiled=True),
        lax.all_gather(w_down, "shard", axis=0, tiled=True),
        lax.all_gather(gain_ffn, "shard", axis=0, tiled=True),
    )
    full_gate, full_up, full_down, full_gffn = ffn_set
    normed_mid, unit_mid, rms_mid = norm_rows(resid_mid, full_gffn)
    hidden_in = normed_mid.astype(jnp.bfloat16)
    gate_proj = matmul(hidden_in, full_gate)
    up_proj = matmul(hidden_in, full_up)
    gate_sig = jax.nn.sigmoid(gate_proj)
    gate_act = gate_proj * gate_sig
    hidden_bf = (gate_act * up_proj).astype(jnp.bfloat16)
    block_out = (resid_mid + matmul(hidden_bf, full_down)).astype(jnp.bfloat16)
    back_gate, back_up, back_down, back_gffn = (
        lax.all_gather(w_gate, "shard", axis=0, tiled=True),
        lax.all_gather(w_up, "shard", axis=0, tiled=True),
        lax.all_gather(w_down, "shard", axis=0, tiled=True),
        lax.all_gather(gain_ffn, "shard", axis=0, tiled=True),
    )
    live_rows = (doc_ids >= 0).astype(jnp.float32)[:, None]
    grad_y = cotangent.astype(jnp.float32) * live_rows
    grad_y_bf = grad_y.astype(jnp.bfloat16)
    part_down = matmul(hidden_bf.T, grad_y_bf)
    grad_down = lax.psum_scatter(
        part_down.astype(jnp.bfloat16), "shard", scatter_dimension=0, tiled=True
    ).astype(jnp.float32)
    grad_down = lax.psum(grad_down.astype(jnp.bfloat16), "rep").astype(jnp.float32)
    grad_hidden = matmul(grad_y_bf, back_down.T)
    grad_gate_bf = (grad_hidden * up_proj * gate_sig * (1.0 + gate_proj * (1.0 - gate_sig))).astype(
        jnp.bfloat16
    )
    grad_up_bf = (grad_hidden * gate_act).astype(jnp.bfloat16)
    part_gate = matmul(hidden_in.T, grad_gate_bf)
    part_up = matmul(hidden_in.T, grad_up_bf)
    grad_norm_mid = matmul(grad_gate_bf, back_gate.T) + matmul(grad_up_bf, back_up.T)
    back_mid, part_gffn = norm_back(grad_norm_mid, unit_mid, rms_mid, back_gffn)
    grad_gate, grad_up, grad_gffn = (
        lax.psum_scatter(
            part_gate.astype(jnp.bfloat16), "shard", scatter_dimension=0, tiled=True
        ).astype(jnp.float32),
        lax.psum_scatter(
            part_up.astype(jnp.bfloat16), "shard", scatter_dimension=0, tiled=True
        ).astype(jnp.float32),
        lax.psum_scatter(
            part_gffn.astype(jnp.bfloat16), "shard", scatter_dimension=0, tiled=True
        ).astype(jnp.float32),
    )
    grad_gate, grad_up, grad_gffn = (
        lax.psum(grad_gate.astype(jnp.bfloat16), "rep").astype(jnp.float32),
        lax.psum(grad_up.astype(jnp.bfloat16), "rep").astype(jnp.float32),
        lax.psum(grad_gffn.astype(jnp.bfloat16), "rep").astype(jnp.float32),
    )
    grad_mid = grad_y + back_mid
    grad_mid_bf = grad_mid.astype(jnp.bfloat16)
    again_set = (
        lax.all_gather(w_query, "shard", axis=0, tiled=True),
        lax.all_gather(w_key, "shard", axis=0, tiled=True),
        lax.all_gather(w_value, "shard", axis=0, tiled=True),
        lax.all_gather(w_out, "shard", axis=0, tiled=True),
        lax.all_gather(gain_attn, "shard", axis=0, tiled=True),
        lax.all_gather(gain_query, "shard", axis=0, tiled=True),
        lax.all_gather(gain_key, "shard", axis=0, tiled=True),
    )
    back_query, back_key, back_value, back_out, back_gattn, back_gquery, back_gkey = again_set
    part_out = matmul(mixed_bf.T, grad_mid_bf)
    grad_mixed_bf = (
        matmul(grad_mid_bf, back_out.T)
        .astype(jnp.bfloat16)
        .reshape(1, tok_rows, KVH, head_share, HEAD_DIM)
    )
    attn_again, unused_total = attn_probs_of(query_bf, key_bf, key_mask, log_total, score_scale)
    probs_bf = attn_again.astype(jnp.bfloat16)
    grad_scores = jnp.einsum(
        "gqkrd,gskd->gkrqs", grad_mixed_bf, value_bf, preferred_element_type=jnp.float32
    )
    grad_value_bf = (
        jnp.einsum("gkrqs,gqkrd->gskd", probs_bf, grad_mixed_bf, preferred_element_type=jnp.float32)
        .astype(jnp.bfloat16)
        .reshape(tok_rows, KVH * HEAD_DIM)
    )
    row_dot = jnp.sum(attn_again * grad_scores, axis=-1, keepdims=True)
    grad_logits = (attn_again * (grad_scores - row_dot) * score_scale).astype(jnp.bfloat16)
    grad_query_rot = jnp.einsum(
        "gkrqs,gskd->gqkrd", grad_logits, key_bf, preferred_element_type=jnp.float32
    ).reshape(1, tok_rows, QH, HEAD_DIM)
    grad_key_rot = jnp.einsum(
        "gkrqs,gqkrd->gskd", grad_logits, query_bf, preferred_element_type=jnp.float32
    )
    grad_query_raw, part_gquery = norm_back(
        rotate_back(grad_query_rot, cos_tab, sin_tab), query_unit, query_rms, back_gquery
    )
    grad_key_raw, part_gkey = norm_back(
        rotate_back(grad_key_rot, cos_tab, sin_tab), key_unit, key_rms, back_gkey
    )
    grad_query_bf = grad_query_raw.astype(jnp.bfloat16).reshape(tok_rows, QH * HEAD_DIM)
    grad_key_bf = grad_key_raw.astype(jnp.bfloat16).reshape(tok_rows, KVH * HEAD_DIM)
    part_query = matmul(normed_bf.T, grad_query_bf)
    part_key = matmul(normed_bf.T, grad_key_bf)
    part_value = matmul(normed_bf.T, grad_value_bf)
    grad_norm_in = (
        matmul(grad_query_bf, back_query.T)
        + matmul(grad_key_bf, back_key.T)
        + matmul(grad_value_bf, back_value.T)
    )
    back_in, part_gattn = norm_back(grad_norm_in, unit_in, rms_in, back_gattn)
    grad_tokens = grad_mid + back_in
    attn_grads = (
        lax.psum_scatter(
            part_query.astype(jnp.bfloat16), "shard", scatter_dimension=0, tiled=True
        ).astype(jnp.float32),
        lax.psum_scatter(
            part_key.astype(jnp.bfloat16), "shard", scatter_dimension=0, tiled=True
        ).astype(jnp.float32),
        lax.psum_scatter(
            part_value.astype(jnp.bfloat16), "shard", scatter_dimension=0, tiled=True
        ).astype(jnp.float32),
        lax.psum_scatter(
            part_out.astype(jnp.bfloat16), "shard", scatter_dimension=0, tiled=True
        ).astype(jnp.float32),
        lax.psum_scatter(
            part_gattn.astype(jnp.bfloat16), "shard", scatter_dimension=0, tiled=True
        ).astype(jnp.float32),
        lax.psum_scatter(
            part_gquery.astype(jnp.bfloat16), "shard", scatter_dimension=0, tiled=True
        ).astype(jnp.float32),
        lax.psum_scatter(
            part_gkey.astype(jnp.bfloat16), "shard", scatter_dimension=0, tiled=True
        ).astype(jnp.float32),
    )
    grad_query, grad_key, grad_value, grad_out, grad_gattn, grad_gquery, grad_gkey = attn_grads
    grad_query, grad_key, grad_value, grad_out, grad_gattn, grad_gquery, grad_gkey = (
        lax.psum(grad_query.astype(jnp.bfloat16), "rep").astype(jnp.float32),
        lax.psum(grad_key.astype(jnp.bfloat16), "rep").astype(jnp.float32),
        lax.psum(grad_value.astype(jnp.bfloat16), "rep").astype(jnp.float32),
        lax.psum(grad_out.astype(jnp.bfloat16), "rep").astype(jnp.float32),
        lax.psum(grad_gattn.astype(jnp.bfloat16), "rep").astype(jnp.float32),
        lax.psum(grad_gquery.astype(jnp.bfloat16), "rep").astype(jnp.float32),
        lax.psum(grad_gkey.astype(jnp.bfloat16), "rep").astype(jnp.float32),
    )
    return (
        block_out,
        grad_tokens,
        grad_query,
        grad_key,
        grad_value,
        grad_out,
        grad_gate,
        grad_up,
        grad_down,
        grad_gattn,
        grad_gffn,
        grad_gquery,
        grad_gkey,
    )


def solution(mesh):
    return jax.shard_map(
        local,
        mesh=mesh,
        in_specs=(
            P(("rep", "shard"), None),
            P(("rep", "shard"), None),
            P(("rep", "shard")),
            P("shard", None),
            P("shard", None),
            P("shard", None),
            P("shard", None),
            P("shard", None),
            P("shard", None),
            P("shard", None),
            P("shard"),
            P("shard"),
            P("shard"),
            P("shard"),
        ),
        out_specs=(
            P(("rep", "shard"), None),
            P(("rep", "shard"), None),
            P("shard", None),
            P("shard", None),
            P("shard", None),
            P("shard", None),
            P("shard", None),
            P("shard", None),
            P("shard", None),
            P("shard"),
            P("shard"),
            P("shard"),
            P("shard"),
        ),
        check_vma=False,
    )
```

profile of v0, /device:TPU:0, one launch (start us, length us, event | category | flops | bytes accessed | tf_op | source)
XLA Modules:
  0.0 995.9 jit_solution(12376034962835203929)
XLA Ops:
  12.0 6.0 all-gather
  19.8 8.2 all-reduce.9
  38.2 9.2 all-gather.10.cloned.1.call-done
  50.8 20.9 %all-gather.14.cloned.1.call-done = bf16[1024,1024]{1,0:T(8,128)(2,1)} async-done(((bf16[256,1024]{1,0:T(8,128)(2,1)}), bf16[1024,1024]{1,0:T(8,128)(2,1)}) %all-gather.14.cloned.1.call-update) | async-done | bytes 2097168 | tf_op jit(solution)/shard_map/all_gather | solution.py:105
  75.9 19.7 %all-gather.16.cloned.1.call-done = bf16[1024,1024]{1,0:T(8,128)(2,1)} async-done(((bf16[256,1024]{1,0:T(8,128)(2,1)}), bf16[1024,1024]{1,0:T(8,128)(2,1)}) %all-gather.16.cloned.1.call-update) | async-done | bytes 2097168 | tf_op jit(solution)/shard_map/all_gather | solution.py:108
  98.0 63.3 %all-gather.18.cloned.1.call-done = bf16[1024,4608]{1,0:T(8,128)(2,1)} async-done(((bf16[256,4608]{1,0:T(8,128)(2,1)}), bf16[1024,4608]{1,0:T(8,128)(2,1)}) %all-gather.18.cloned.1.call-update) | async-done | bytes 9437200 | tf_op jit(solution)/shard_map/all_gather | solution.py:143
  161.3 6.5 fusion.45
  167.8 59.2 %all-gather.20.cloned.1.call-done = bf16[1024,4608]{1,0:T(8,128)(2,1)} async-done(((bf16[256,4608]{1,0:T(8,128)(2,1)}), bf16[1024,4608]{1,0:T(8,128)(2,1)}) %all-gather.20.cloned.1.call-update) | async-done | bytes 9437200 | tf_op jit(solution)/shard_map/all_gather | solution.py:144
  227.0 6.5 fusion.46
  233.5 59.3 %all-gather.22.cloned.1.call-done = bf16[4608,1024]{1,0:T(8,128)(2,1)} async-done(((bf16[1152,1024]{1,0:T(8,128)(2,1)}), bf16[4608,1024]{1,0:T(8,128)(2,1)}) %all-gather.22.cloned.1.call-update) | async-done | bytes 9437200 | tf_op jit(solution)/shard_map/all_gather | solution.py:145
  292.8 8.8 multiply_convert_fusion
  301.6 7.6 fusion.47
  347.3 6.4 convolution_convert_fusion.2
  353.8 6.3 convolution_convert_fusion.1
  366.4 16.8 %reduce-scatter.12.cloned.1.call-done = bf16[256,512]{1,0:T(8,128)(2,1)} async-done(((bf16[1024,512]{1,0:T(8,128)(2,1)}), bf16[256,512]{1,0:T(8,128)(2,1)}) %reduce-scatter.12.cloned.1.call-update) | async-done | bytes 262160 | tf_op jit(solution)/shard_map/reduce_scatter | solution.py:257
  383.3 34.1 %reduce-scatter.8.cloned.1.call-done = bf16[256,1024]{1,0:T(8,128)(2,1)} async-done(((bf16[1024,1024]{1,0:T(8,128)(2,1)}), bf16[256,1024]{1,0:T(8,128)(2,1)}) %reduce-scatter.8.cloned.1.call-update) | async-done | bytes 524304 | tf_op jit(solution)/shard_map/reduce_scatter | solution.py:251
  417.4 34.3 %reduce-scatter.14.cloned.1.call-done = bf16[256,1024]{1,0:T(8,128)(2,1)} async-done(((bf16[1024,1024]{1,0:T(8,128)(2,1)}), bf16[256,1024]{1,0:T(8,128)(2,1)}) %reduce-scatter.14.cloned.1.call-update) | async-done | bytes 524304 | tf_op jit(solution)/shard_map/reduce_scatter | solution.py:260
  451.7 80.4 %reduce-scatter.16.cloned.1.call-done = bf16[256,4608]{1,0:T(8,128)(2,1)} async-done(((bf16[1024,4608]{1,0:T(8,128)(2,1)}), bf16[256,4608]{1,0:T(8,128)(2,1)}) %reduce-scatter.16.cloned.1.call-update) | async-done | bytes 2359312 | tf_op jit(solution)/shard_map/reduce_scatter | solution.py:181
  532.1 80.5 %reduce-scatter.18.cloned.1.call-done = bf16[256,4608]{1,0:T(8,128)(2,1)} async-done(((bf16[1024,4608]{1,0:T(8,128)(2,1)}), bf16[256,4608]{1,0:T(8,128)(2,1)}) %reduce-scatter.18.cloned.1.call-update) | async-done | bytes 2359312 | tf_op jit(solution)/shard_map/reduce_scatter | solution.py:184
  612.6 80.4 %reduce-scatter.20.cloned.1.call-done = bf16[1152,1024]{1,0:T(8,128)(2,1)} async-done(((bf16[4608,1024]{1,0:T(8,128)(2,1)}), bf16[1152,1024]{1,0:T(8,128)(2,1)}) %reduce-scatter.20.cloned.1.call-update) | async-done | bytes 2359312 | tf_op jit(solution)/shard_map/reduce_scatter | solution.py:167
  699.5 5.8 all-reduce.8
  705.6 23.1 %all-reduce.6 = (bf16[256]{0:T(256)(128)(2,1)S(1)}, bf16[256]{0:T(256)(128)(2,1)S(1)}, bf16[16]{0:T(256)(128)(2,1)S(1)}, bf16[16]{0:T(256)(128)(2,1)S(1)}) all-reduce(bf16[256]{0:T(256)(128)(2,1)S(1)} %dynamic-slice.3, bf16[256]{0:T(256)(128)(2,1)S(1)} %dynamic-slice.5, ...), channel_id=1, replica_groups=mesh['rep'=8,'shard'=4] {'rep'}, use_global_device_ids=true, to_apply=%region_27.28 | all-reduce | flops 544 | bytes 2176 | tf_op jit(solution)/shard_map/psum | solution.py:279
  731.9 5.8 fusion.2
  737.7 237.7 %all-reduce.12.cloned.1.call-done = (bf16[256,1024]{1,0:T(8,128)(2,1)}, bf16[256,512]{1,0:T(8,128)(2,1)}, bf16[256,512]{1,0:T(8,128)(2,1)}, bf16[256,1024]{1,0:T...) async-done(((bf16[256,1024]{1,0:T(8,128)(2,1)}, bf16[256,512]{1,0:T(8,128)(2,1)}, bf16[256,512]{1,0:T(8,128)(2,1)}, ...) | async-done | bytes 8650768 | tf_op jit(solution)/shard_map/psum | solution.py:275
  (283 shorter events, 91.9 us)
Async XLA Ops:
  7.2 29.2 %all-gather.12.cloned.1.call-start = ((), (), s32[]{:S(2)}) async-start(), calls=%async_computation.8 | async-start | bytes 1310720 | tf_op jit(solution)/shard_map/all_gather | solution.py:106
  7.9 39.5 %all-gather.10.cloned.1.call-start = ((), (), s32[]{:S(2)}) async-start(), calls=%async_computation.7 | async-start | bytes 1310720 | tf_op jit(solution)/shard_map/all_gather | solution.py:107
  8.7 63.0 %all-gather.14.cloned.1.call-start = ((), (), s32[]{:S(2)}) async-start(), calls=%async_computation.9 | async-start | bytes 2621440 | tf_op jit(solution)/shard_map/all_gather | solution.py:105
  9.4 86.3 %all-gather.16.cloned.1.call-start = ((), (), s32[]{:S(2)}) async-start(), calls=%async_computation.10 | async-start | bytes 2621440 | tf_op jit(solution)/shard_map/all_gather | solution.py:108
  10.0 151.3 %all-gather.18.cloned.1.call-start = ((), (), s32[]{:S(2)}) async-start(), calls=%async_computation.11 | async-start | bytes 11796480 | tf_op jit(solution)/shard_map/all_gather | solution.py:143
  10.6 24.3 %copy-start.1 = (bf16[128,1024]{1,0:T(8,128)(2,1)S(1)}, bf16[128,1024]{1,0:T(8,128)(2,1)}, u32[]{:S(2)}) copy-start(bf16[128,1024]{1,0:T(8,128)(2,1)} %param.14) | copy-start | bytes 786436
  10.6 216.3 %all-gather.20.cloned.1.call-start = ((), (), s32[]{:S(2)}) async-start(), calls=%async_computation.12 | async-start | bytes 11796480 | tf_op jit(solution)/shard_map/all_gather | solution.py:144
  11.2 281.6 %all-gather.22.cloned.1.call-start = ((), (), s32[]{:S(2)}) async-start(), calls=%async_computation.13 | async-start | bytes 11796480 | tf_op jit(solution)/shard_map/all_gather | solution.py:145
  12.0 354.5 %reduce-scatter.10.cloned.1.call-start = ((), (), s32[]{:S(2)}) async-start(), calls=%async_computation.15 | async-start | bytes 1310720 | tf_op jit(solution)/shard_map/reduce_scatter | solution.py:254
  18.1 53.6 %copy-start.38 = (f32[4,1,256]{2,1,0:T(1,128)}, f32[4,1,256]{2,1,0:T(1,128)S(1)}, u32[]{:S(2)}) copy-start(f32[4,1,256]{2,1,0:T(1,128)S(1)} %convert_element_type.270) | copy-start | bytes 12292
  28.1 46.0 %copy-start.63 = (f32[64]{0:T(128)}, f32[64]{0:T(128)S(1)}, u32[]{:S(2)}) copy-start(f32[64]{0:T(128)S(1)} %convert_element_type.226) | copy-start | bytes 772
  35.5 36.1 %copy-start.54 = (f32[128]{0:T(128)}, f32[128]{0:T(128)S(1)}, u32[]{:S(2)}) copy-start(f32[128]{0:T(128)S(1)} %add_rsqrt_fusion.3) | copy-start | bytes 1540
  36.4 38.4 %copy-start.33 = (f32[128,32]{0,1:T(8,128)}, f32[128,32]{0,1:T(8,128)S(1)}, u32[]{:S(2)}) copy-start(f32[128,32]{0,1:T(8,128)S(1)} %get-tuple-element.54) | copy-start | bytes 49156
  38.1 35.7 %copy-start.17 = (f32[128,512]{1,0:T(8,128)}, f32[128,512]{1,0:T(8,128)S(1)}, u32[]{:S(2)}) copy-start(f32[128,512]{1,0:T(8,128)S(1)} %fusion.41) | copy-start | bytes 786436
  49.1 26.5 %copy-start.20 = (bf16[128,512]{0,1:T(8,128)(2,1)}, bf16[128,512]{0,1:T(8,128)(2,1)S(1)}, u32[]{:S(2)}) copy-start(bf16[128,512]{0,1:T(8,128)(2,1)S(1)} %copy.81) | copy-start | bytes 393220
  49.1 24.8 %copy-start.52 = (f32[128,8]{0,1:T(8,128)}, f32[128,8]{0,1:T(8,128)S(1)}, u32[]{:S(2)}) copy-start(f32[128,8]{0,1:T(8,128)S(1)} %add_rsqrt_fusion.1) | copy-start | bytes 12292
  97.8 70.0 %copy-start.59 = (f32[128]{0:T(128)}, f32[128]{0:T(128)S(1)}, u32[]{:S(2)}) copy-start(f32[128]{0:T(128)S(1)} %add_rsqrt_fusion.2) | copy-start | bytes 1540
  330.4 52.9 %reduce-scatter.12.cloned.1.call-start = ((), (), s32[]{:S(2)}) async-start(), calls=%async_computation.16 | async-start | bytes 1310720 | tf_op jit(solution)/shard_map/reduce_scatter | solution.py:257
  334.3 83.1 %reduce-scatter.8.cloned.1.call-start = ((), (), s32[]{:S(2)}) async-start(), calls=%async_computation.14 | async-start | bytes 2621440 | tf_op jit(solution)/shard_map/reduce_scatter | solution.py:251
  345.2 106.5 %reduce-scatter.14.cloned.1.call-start = ((), (), s32[]{:S(2)}) async-start(), calls=%async_computation.17 | async-start | bytes 2621440 | tf_op jit(solution)/shard_map/reduce_scatter | solution.py:260
  347.3 184.8 %reduce-scatter.16.cloned.1.call-start = ((), (), s32[]{:S(2)}) async-start(), calls=%async_computation.18 | async-start | bytes 11796480 | tf_op jit(solution)/shard_map/reduce_scatter | solution.py:181
  353.7 258.9 %reduce-scatter.18.cloned.1.call-start = ((), (), s32[]{:S(2)}) async-start(), calls=%async_computation.19 | async-start | bytes 11796480 | tf_op jit(solution)/shard_map/reduce_scatter | solution.py:184
  360.2 332.9 %reduce-scatter.20.cloned.1.call-start = ((), (), s32[]{:S(2)}) async-start(), calls=%async_computation.20 | async-start | bytes 11796480 | tf_op jit(solution)/shard_map/reduce_scatter | solution.py:167
  366.4 609.1 %all-reduce.12.cloned.1.call-start = ((), (), s32[]{:S(2)}) async-start(), calls=%async_computation.21 | async-start | bytes 17301504 | tf_op jit(solution)/shard_map/psum | solution.py:275
  (66 other events, 329.5 us)
Sparse Core Ops, SparseCore 0:
  9.5 19.4 all-gather.11
  30.6 16.6 all-gather.9
  48.9 22.6 all-gather.13
  73.1 22.5 all-gather.15
  97.1 64.2 all-gather.17
  162.7 64.2 all-gather.19
  228.5 64.2 all-gather.21
  330.5 24.8 reduce-scatter.9
  358.5 24.7 reduce-scatter.11
  386.2 31.1 reduce-scatter.7
  420.5 31.1 reduce-scatter.13
  454.2 77.8 reduce-scatter.15
  534.7 77.8 reduce-scatter.17
  615.1 77.8 reduce-scatter.19
  698.4 277.0 all-reduce.11
where the time goes:
time: 997 us; the launch traced here: 996 us
  waiting for transfers between devices  800 us (80%)
  matrix products  83.1 us (8%)
  blocking collectives  48.2 us (5%)
  other arithmetic  26.1 us (3%)
  local copies, waits for them, and re-layouts  20.5 us (2%)
  between operations  17 us (2%)
    psum x1, waiting for transfers between devices, local(): lax.psum(grad_query.astype(jnp.bfloat16), 'rep').astype(jnp.float32)  238 us
    reduce_scatter x1, waiting for transfers between devices, local(): lax.psum_scatter(part_up.astype(jnp.bfloat16), 'shard', scatter_dimension...  80.5 us
    reduce_scatter x1, waiting for transfers between devices, local(): lax.psum_scatter(part_gate.astype(jnp.bfloat16), 'shard', scatter_dimensi...  80.4 us
    reduce_scatter x1, waiting for transfers between devices, local(): lax.psum_scatter(part_down.astype(jnp.bfloat16), 'shard', scatter_dimensi...  80.4 us
    dot_general x21, matrix products, matmul(): return jnp.dot(left, right, preferred_element_type=jnp.float32)  79.3 us
    all_gather x1, waiting for transfers between devices, local(): lax.all_gather(w_gate, 'shard', axis=0, tiled=True)  63.3 us
    all_gather x1, waiting for transfers between devices, local(): lax.all_gather(w_down, 'shard', axis=0, tiled=True)  59.3 us
    all_gather x1, waiting for transfers between devices, local(): lax.all_gather(w_up, 'shard', axis=0, tiled=True)  59.2 us
  transfers between devices with their start and end apart: 15, of which 13 were waited for; matrix products, arithmetic and copies ran while one was open for 8% of the time, Pallas kernels for 0%

commit v1 on v0

--- a/solution.py
+++ b/solution.py
@@ -272,7 +272,7 @@
     )
     grad_query, grad_key, grad_value, grad_out, grad_gattn, grad_gquery, grad_gkey = attn_grads
     grad_query, grad_key, grad_value, grad_out, grad_gattn, grad_gquery, grad_gkey = (
-        lax.psum(grad_query.astype(jnp.bfloat16), "rep").astype(jnp.float32),
+        jnp.sum(lax.all_gather(grad_query.astype(jnp.bfloat16), "rep"), axis=0).astype(jnp.float32),
         lax.psum(grad_key.astype(jnp.bfloat16), "rep").astype(jnp.float32),
         lax.psum(grad_value.astype(jnp.bfloat16), "rep").astype(jnp.float32),
         lax.psum(grad_out.astype(jnp.bfloat16), "rep").astype(jnp.float32),

time: 997 us -> 1060 us (1.063)
  waiting for transfers between devices: 800 us -> 848 us
    reduce_scatter x1, waiting for transfers between devices: 34.1 us -> 0.02 us  [local(): lax.psum_scatter(part_query.astype(jnp.bfloat16), 'shard', scatter_dimens...]
    all_gather x0 -> x1, waiting for transfers between devices: none -> 31.2 us  [local(): lax.all_gather(grad_query.astype(jnp.bfloat16), 'rep')]
    psum x1, waiting for transfers between devices: 238 us -> 262 us  [local(): lax.psum(grad_key.astype(jnp.bfloat16), 'rep').astype(jnp.float32)]
    reduce_scatter x1, waiting for transfers between devices: 0.02 us -> 15 us  [local(): lax.psum_scatter(part_key.astype(jnp.bfloat16), 'shard', scatter_dimensio...]
    reduce_scatter x1, waiting for transfers between devices: 16.8 us -> 27.7 us  [local(): lax.psum_scatter(part_value.astype(jnp.bfloat16), 'shard', scatter_dimens...]
  transfers between devices with their start and end apart: 15 -> 16, of which waited for: 13 -> 14; matrix products, arithmetic and copies ran while one was open for 8% -> 8% of each run, Pallas kernels for 0% -> 0%
where the time goes in v1:
time: 1060 us; the launch traced here: 1050 us
  waiting for transfers between devices  848 us (80%)
  matrix products  84.2 us (8%)
  blocking collectives  47.4 us (4%)
  other arithmetic  31.5 us (3%)
  local copies, waits for them, and re-layouts  25.8 us (2%)
  between operations  16.9 us (2%)
    psum x1, waiting for transfers between devices, local(): lax.psum(grad_key.astype(jnp.bfloat16), 'rep').astype(jnp.float32)  262 us
    reduce_scatter x1, waiting for transfers between devices, local(): lax.psum_scatter(part_up.astype(jnp.bfloat16), 'shard', scatter_dimension...  80.6 us
    reduce_scatter x1, waiting for transfers between devices, local(): lax.psum_scatter(part_gate.astype(jnp.bfloat16), 'shard', scatter_dimensi...  80.4 us
    reduce_scatter x1, waiting for transfers between devices, local(): lax.psum_scatter(part_down.astype(jnp.bfloat16), 'shard', scatter_dimensi...  80.4 us
    dot_general x21, matrix products, matmul(): return jnp.dot(left, right, preferred_element_type=jnp.float32)  79.3 us
    all_gather x1, waiting for transfers between devices, local(): lax.all_gather(w_gate, 'shard', axis=0, tiled=True)  63.4 us
    all_gather x1, waiting for transfers between devices, local(): lax.all_gather(w_down, 'shard', axis=0, tiled=True)  59.3 us
    all_gather x1, waiting for transfers between devices, local(): lax.all_gather(w_up, 'shard', axis=0, tiled=True)  59.2 us
  transfers between devices with their start and end apart: 16, of which 14 were waited for; matrix products, arithmetic and copies ran while one was open for 8% of the time, Pallas kernels for 0%

profile of v1, /device:TPU:0, one launch (start us, length us, event | category | flops | bytes accessed | tf_op | source)
XLA Modules:
  0.0 1054.9 jit_solution(10964151992335791158)
XLA Ops:
  12.0 6.0 all-gather.1
  19.8 8.2 all-reduce.9
  38.2 9.1 all-gather.12.cloned.1.call-done
  50.0 21.6 %all-gather.16.cloned.1.call-done = bf16[1024,1024]{1,0:T(8,128)(2,1)} async-done(((bf16[256,1024]{1,0:T(8,128)(2,1)}), bf16[1024,1024]{1,0:T(8,128)(2,1)}) %all-gather.16.cloned.1.call-update) | async-done | bytes 2097168 | tf_op jit(solution)/shard_map/all_gather | solution.py:105
  76.8 18.7 %all-gather.18.cloned.1.call-done = bf16[1024,1024]{1,0:T(8,128)(2,1)} async-done(((bf16[256,1024]{1,0:T(8,128)(2,1)}), bf16[1024,1024]{1,0:T(8,128)(2,1)}) %all-gather.18.cloned.1.call-update) | async-done | bytes 2097168 | tf_op jit(solution)/shard_map/all_gather | solution.py:108
  97.9 63.4 %all-gather.20.cloned.1.call-done = bf16[1024,4608]{1,0:T(8,128)(2,1)} async-done(((bf16[256,4608]{1,0:T(8,128)(2,1)}), bf16[1024,4608]{1,0:T(8,128)(2,1)}) %all-gather.20.cloned.1.call-update) | async-done | bytes 9437200 | tf_op jit(solution)/shard_map/all_gather | solution.py:143
  161.2 6.5 fusion.45
  167.7 59.2 %all-gather.22.cloned.1.call-done = bf16[1024,4608]{1,0:T(8,128)(2,1)} async-done(((bf16[256,4608]{1,0:T(8,128)(2,1)}), bf16[1024,4608]{1,0:T(8,128)(2,1)}) %all-gather.22.cloned.1.call-update) | async-done | bytes 9437200 | tf_op jit(solution)/shard_map/all_gather | solution.py:144
  226.9 6.5 fusion.46
  233.4 59.3 %all-gather.24.cloned.1.call-done = bf16[4608,1024]{1,0:T(8,128)(2,1)} async-done(((bf16[1152,1024]{1,0:T(8,128)(2,1)}), bf16[4608,1024]{1,0:T(8,128)(2,1)}) %all-gather.24.cloned.1.call-update) | async-done | bytes 9437200 | tf_op jit(solution)/shard_map/all_gather | solution.py:145
  292.7 8.8 multiply_convert_fusion
  301.5 7.6 fusion.47
  355.7 6.4 convolution_convert_fusion.2
  362.1 6.4 convolution_convert_fusion.1
  375.3 15.0 %reduce-scatter.10.cloned.1.call-done = bf16[256,512]{1,0:T(8,128)(2,1)} async-done(((bf16[1024,512]{1,0:T(8,128)(2,1)}), bf16[256,512]{1,0:T(8,128)(2,1)}) %reduce-scatter.10.cloned.1.call-update) | async-done | bytes 262160 | tf_op jit(solution)/shard_map/reduce_scatter | solution.py:254
  390.3 27.7 %reduce-scatter.12.cloned.1.call-done = bf16[256,512]{1,0:T(8,128)(2,1)} async-done(((bf16[1024,512]{1,0:T(8,128)(2,1)}), bf16[256,512]{1,0:T(8,128)(2,1)}) %reduce-scatter.12.cloned.1.call-update) | async-done | bytes 262160 | tf_op jit(solution)/shard_map/reduce_scatter | solution.py:257
  418.1 34.3 %reduce-scatter.14.cloned.1.call-done = bf16[256,1024]{1,0:T(8,128)(2,1)} async-done(((bf16[1024,1024]{1,0:T(8,128)(2,1)}), bf16[256,1024]{1,0:T(8,128)(2,1)}) %reduce-scatter.14.cloned.1.call-update) | async-done | bytes 524304 | tf_op jit(solution)/shard_map/reduce_scatter | solution.py:260
  452.4 80.4 %reduce-scatter.16.cloned.1.call-done = bf16[256,4608]{1,0:T(8,128)(2,1)} async-done(((bf16[1024,4608]{1,0:T(8,128)(2,1)}), bf16[256,4608]{1,0:T(8,128)(2,1)}) %reduce-scatter.16.cloned.1.call-update) | async-done | bytes 2359312 | tf_op jit(solution)/shard_map/reduce_scatter | solution.py:181
  532.8 80.6 %reduce-scatter.18.cloned.1.call-done = bf16[256,4608]{1,0:T(8,128)(2,1)} async-done(((bf16[1024,4608]{1,0:T(8,128)(2,1)}), bf16[256,4608]{1,0:T(8,128)(2,1)}) %reduce-scatter.18.cloned.1.call-update) | async-done | bytes 2359312 | tf_op jit(solution)/shard_map/reduce_scatter | solution.py:184
  613.4 80.4 %reduce-scatter.20.cloned.1.call-done = bf16[1152,1024]{1,0:T(8,128)(2,1)} async-done(((bf16[4608,1024]{1,0:T(8,128)(2,1)}), bf16[1152,1024]{1,0:T(8,128)(2,1)}) %reduce-scatter.20.cloned.1.call-update) | async-done | bytes 2359312 | tf_op jit(solution)/shard_map/reduce_scatter | solution.py:167
  700.3 5.8 all-reduce.8
  706.5 22.3 %all-reduce.6 = (bf16[256]{0:T(256)(128)(2,1)S(1)}, bf16[256]{0:T(256)(128)(2,1)S(1)}, bf16[16]{0:T(256)(128)(2,1)S(1)}, bf16[16]{0:T(256)(128)(2,1)S(1)}) all-reduce(bf16[256]{0:T(256)(128)(2,1)S(1)} %dynamic-slice.3, bf16[256]{0:T(256)(128)(2,1)S(1)} %dynamic-slice.5, ...), channel_id=1, replica_groups=mesh['rep'=8,'shard'=4] {'rep'}, use_global_device_ids=true, to_apply=%region_27.28 | all-reduce | flops 544 | bytes 2176 | tf_op jit(solution)/shard_map/psum | solution.py:279
  737.7 31.2 %all-gather.26.cloned.1.call-done = bf16[2048,1024]{1,0:T(8,128)(2,1)} async-done(((bf16[256,1024]{1,0:T(8,128)(2,1)}), bf16[2048,1024]{1,0:T(8,128)(2,1)}) %all-gather.26.cloned.1.call-update) | async-done | bytes 4194320 | tf_op jit(solution)/shard_map/all_gather | solution.py:275
  773.1 262.5 %all-reduce.12.cloned.1.call-done = (bf16[256,512]{1,0:T(8,128)(2,1)}, bf16[256,512]{1,0:T(8,128)(2,1)}, bf16[256,1024]{1,0:T(8,128)(2,1)}, bf16[256,4608]{1,0:T...) async-done(((bf16[256,512]{1,0:T(8,128)(2,1)}, bf16[256,512]{1,0:T(8,128)(2,1)}, bf16[256,1024]{1,0:T(8,128)(2,1)}, bf16[256,4608]{1,0:T(8,128)(2,1)}, ...) | async-done | bytes 8126480 | tf_op jit(solution)/shard_map/psum | solution.py:276
  (281 shorter events, 110.1 us)
Async XLA Ops:
  7.2 29.3 %all-gather.14.cloned.1.call-start = ((), (), s32[]{:S(2)}) async-start(), calls=%async_computation.8 | async-start | bytes 1310720 | tf_op jit(solution)/shard_map/all_gather | solution.py:106
  7.9 39.5 %all-gather.12.cloned.1.call-start = ((), (), s32[]{:S(2)}) async-start(), calls=%async_computation.7 | async-start | bytes 1310720 | tf_op jit(solution)/shard_map/all_gather | solution.py:107
  8.7 62.9 %all-gather.16.cloned.1.call-start = ((), (), s32[]{:S(2)}) async-start(), calls=%async_computation.9 | async-start | bytes 2621440 | tf_op jit(solution)/shard_map/all_gather | solution.py:105
  9.4 86.2 %all-gather.18.cloned.1.call-start = ((), (), s32[]{:S(2)}) async-start(), calls=%async_computation.10 | async-start | bytes 2621440 | tf_op jit(solution)/shard_map/all_gather | solution.py:108
  10.0 151.2 %all-gather.20.cloned.1.call-start = ((), (), s32[]{:S(2)}) async-start(), calls=%async_computation.11 | async-start | bytes 11796480 | tf_op jit(solution)/shard_map/all_gather | solution.py:143
  10.6 216.2 %all-gather.22.cloned.1.call-start = ((), (), s32[]{:S(2)}) async-start(), calls=%async_computation.12 | async-start | bytes 11796480 | tf_op jit(solution)/shard_map/all_gather | solution.py:144
  11.2 281.5 %all-gather.24.cloned.1.call-start = ((), (), s32[]{:S(2)}) async-start(), calls=%async_computation.13 | async-start | bytes 11796480 | tf_op jit(solution)/shard_map/all_gather | solution.py:145
  12.0 362.8 %reduce-scatter.8.cloned.1.call-start = ((), (), s32[]{:S(2)}) async-start(), calls=%async_computation.14 | async-start | bytes 2621440 | tf_op jit(solution)/shard_map/reduce_scatter | solution.py:251
  18.1 53.5 %copy-start.36 = (f32[4,1,256]{2,1,0:T(1,128)}, f32[4,1,256]{2,1,0:T(1,128)S(1)}, u32[]{:S(2)}) copy-start(f32[4,1,256]{2,1,0:T(1,128)S(1)} %convert_element_type.272) | copy-start | bytes 12292
  28.1 45.9 %copy-start.62 = (f32[64]{0:T(128)}, f32[64]{0:T(128)S(1)}, u32[]{:S(2)}) copy-start(f32[64]{0:T(128)S(1)} %convert_element_type.228) | copy-start | bytes 772
  35.6 36.0 %copy-start.52 = (f32[128]{0:T(128)}, f32[128]{0:T(128)S(1)}, u32[]{:S(2)}) copy-start(f32[128]{0:T(128)S(1)} %add_rsqrt_fusion.3) | copy-start | bytes 1540
  36.4 37.7 %copy-start.30 = (f32[128,32]{0,1:T(8,128)}, f32[128,32]{0,1:T(8,128)S(1)}, u32[]{:S(2)}) copy-start(f32[128,32]{0,1:T(8,128)S(1)} %get-tuple-element.53) | copy-start | bytes 49156
  38.1 33.5 %copy-start.17 = (f32[128,512]{1,0:T(8,128)}, f32[128,512]{1,0:T(8,128)S(1)}, u32[]{:S(2)}) copy-start(f32[128,512]{1,0:T(8,128)S(1)} %fusion.41) | copy-start | bytes 786436
  49.1 27.4 %copy-start.20 = (bf16[128,512]{0,1:T(8,128)(2,1)}, bf16[128,512]{0,1:T(8,128)(2,1)S(1)}, u32[]{:S(2)}) copy-start(bf16[128,512]{0,1:T(8,128)(2,1)S(1)} %copy.81) | copy-start | bytes 393220
  76.8 90.9 %copy-start.18 = (bf16[8,64,2,128]{3,1,2,0:T(8,128)(2,1)}, bf16[8,64,2,128]{3,1,2,0:T(8,128)(2,1)S(1)}, u32[]{:S(2)}) copy-start(bf16[8,64,2,128]{3,1,2,0:T(8,128)(2,1)S(1)} %convolution_convert_fusion.8) | copy-start | bytes 786436
  97.7 70.0 %copy-start.58 = (f32[128]{0:T(128)}, f32[128]{0:T(128)S(1)}, u32[]{:S(2)}) copy-start(f32[128]{0:T(128)S(1)} %add_rsqrt_fusion.2) | copy-start | bytes 1540
  331.0 59.3 %reduce-scatter.10.cloned.1.call-start = ((), (), s32[]{:S(2)}) async-start(), calls=%async_computation.15 | async-start | bytes 1310720 | tf_op jit(solution)/shard_map/reduce_scatter | solution.py:254
  349.6 68.5 %reduce-scatter.12.cloned.1.call-start = ((), (), s32[]{:S(2)}) async-start(), calls=%async_computation.16 | async-start | bytes 1310720 | tf_op jit(solution)/shard_map/reduce_scatter | solution.py:257
  353.5 98.9 %reduce-scatter.14.cloned.1.call-start = ((), (), s32[]{:S(2)}) async-start(), calls=%async_computation.17 | async-start | bytes 2621440 | tf_op jit(solution)/shard_map/reduce_scatter | solution.py:260
  355.6 177.2 %reduce-scatter.16.cloned.1.call-start = ((), (), s32[]{:S(2)}) async-start(), calls=%async_computation.18 | async-start | bytes 11796480 | tf_op jit(solution)/shard_map/reduce_scatter | solution.py:181
  362.1 251.3 %reduce-scatter.18.cloned.1.call-start = ((), (), s32[]{:S(2)}) async-start(), calls=%async_computation.19 | async-start | bytes 11796480 | tf_op jit(solution)/shard_map/reduce_scatter | solution.py:184
  368.5 325.3 %reduce-scatter.20.cloned.1.call-start = ((), (), s32[]{:S(2)}) async-start(), calls=%async_computation.20 | async-start | bytes 11796480 | tf_op jit(solution)/shard_map/reduce_scatter | solution.py:167
  374.7 394.2 %all-gather.26.cloned.1.call-start = ((), (), s32[]{:S(2)}) async-start(), calls=%async_computation.21 | async-start | bytes 4718592 | tf_op jit(solution)/shard_map/all_gather | solution.py:275
  375.3 660.3 %all-reduce.12.cloned.1.call-start = ((), (), s32[]{:S(2)}) async-start(), calls=%async_computation.22 | async-start | bytes 16252928 | tf_op jit(solution)/shard_map/psum | solution.py:276
  (64 other events, 330.6 us)
Sparse Core Ops, SparseCore 0:
  9.5 19.4 all-gather.13
  30.6 16.6 all-gather.11
  48.9 22.5 all-gather.15
  73.0 22.5 all-gather.17
  97.0 64.2 all-gather.19
  162.6 64.2 all-gather.21
  228.4 64.2 all-gather.23
  331.2 31.1 reduce-scatter.7
  365.5 24.8 reduce-scatter.9
  393.3 24.7 reduce-scatter.11
  421.2 31.1 reduce-scatter.13
  454.8 77.9 reduce-scatter.15
  535.4 77.9 reduce-scatter.17
  615.8 77.9 reduce-scatter.19
  695.8 73.0 all-gather.25
  774.0 261.5 all-reduce.11
